TPU v7x, 32 devices: a whole 2x2x4 slice. The times are simulated.
32 devices in a mesh: grp: 2 (over y), tile: 8 (over z, x), corner: 2 (over core).
Axes of the slice: x: 2, y: 2, z: 4, core: 2. Of those that a mesh axis runs over, the one named last changes fastest.
Arguments:
- mask_logits: float32 [768, 512], P(('grp', 'tile'), 'corner'), parts along dimension 0, may hold values from -1.5 to 1.5
- target: bfloat16 [768, 512], P(('grp', 'tile')), parts along dimension 0, may hold values from 0 to 1
- adam_first: float32 [768, 512], P(('grp', 'tile'), 'corner'), parts along dimension 0, may hold values from -1.5 to 1.5
- adam_second: float32 [768, 512], P(('grp', 'tile'), 'corner'), parts along dimension 0, may hold values from 0.05 to 0.2
- tile_counts: int32 [16, 4], P(('grp', 'tile')), parts along dimension 0, may hold values from 0 to 47
- kernels: float32 [2, 8, 2, 35, 35], P('corner'), may hold values from -0.15625 to 0.15625
- socs_weight: float32 [2, 8], P('corner'), may hold values from 0.03 to 0.3
- corner_dose: float32 [2], P('corner'), may hold values from 0.85 to 1.15
Outputs:
- out_logits: float32 [768, 512], P(('grp', 'tile'), 'corner'), parts along dimension 0
- out_first: float32 [768, 512], P(('grp', 'tile'), 'corner'), parts along dimension 0
- out_second: float32 [768, 512], P(('grp', 'tile'), 'corner'), parts along dimension 0
There are 2 independent parts, one for each index of `grp`. A program takes and returns all parts, laid end to end along the dimension named above; an argument that names none is the same for every part. Nothing has to cross between parts.
All inputs are finite; a program needn't handle non-finite values.
Results may differ from a plain program's by a relative error of at most 0.013.
Values may be sent and summed in bfloat16 or wider, within the bound.
No kernel may reach another device: no remote copies, remote signals or barrier semaphores. Data moves between devices by JAX's collectives and lax.ppermute only.
A program may use at most 64 MiB of HBM per device.

v0:
```python
import math

import jax
import jax.numpy as jnp
from jax import lax
from jax.sharding import PartitionSpec as P

ITERS = 2


steep = 8.0
thresh = 0.5
loss_scale = 20.0
step_size = 0.05
beta_one = 0.9
beta_two = 0.999
adam_eps = 1e-08
prior_steps = 1000.0


def padded(block, sides, width):
    for axis, dim in sides:
        count = lax.axis_size(axis)
        forward = [(i, i + 1) for i in range(count - 1)]
        backward = [(target, source) for source, target in forward]
        low = lax.ppermute(
            lax.slice_in_dim(block, block.shape[dim] - width, None, axis=dim), axis, forward
        )
        high = lax.ppermute(lax.slice_in_dim(block, 0, width, axis=dim), axis, backward)
        block = jnp.concatenate([low, block, high], axis=dim)
    return block


def passed_along(shard, axis, by):
    length = lax.axis_size(axis)
    pairs = [(i, i + by) for i in range(length) if 0 <= i + by < length]
    return lax.ppermute(shard, axis, pairs)


def phase_table(first_index, second_index, length):
    wrapped = jnp.mod(first_index[:, None] * second_index[None, :], length)
    return wrapped.astype(jnp.float32) * (2.0 * math.pi / length)


def dft_tables(strip_rows, kernel_reach, width_all, rows_freq, cols_freq):
    ext_rows = strip_rows + 2 * kernel_reach
    angle_fwd_cols = phase_table(
        jnp.arange(width_all, dtype=jnp.int32), jnp.arange(cols_freq, dtype=jnp.int32), cols_freq
    )
    col_fwd = jnp.concatenate([jnp.cos(angle_fwd_cols), -jnp.sin(angle_fwd_cols)], axis=1).astype(
        jnp.bfloat16
    )
    angle_fwd_rows = phase_table(
        jnp.arange(rows_freq, dtype=jnp.int32), jnp.arange(ext_rows, dtype=jnp.int32), rows_freq
    )
    row_fwd = jnp.concatenate([jnp.cos(angle_fwd_rows), jnp.sin(angle_fwd_rows)], axis=1).astype(
        jnp.bfloat16
    )
    angle_inv_rows = phase_table(
        jnp.arange(strip_rows, dtype=jnp.int32) + kernel_reach,
        jnp.arange(rows_freq, dtype=jnp.int32),
        rows_freq,
    )
    row_inv = jnp.concatenate([jnp.cos(angle_inv_rows), jnp.sin(angle_inv_rows)], axis=1).astype(
        jnp.bfloat16
    )
    angle_inv_cols = phase_table(
        jnp.arange(cols_freq, dtype=jnp.int32), jnp.arange(width_all, dtype=jnp.int32), cols_freq
    )
    cosine_inv = jnp.cos(angle_inv_cols)
    sine_inv = jnp.sin(angle_inv_cols)
    upper_block = jnp.concatenate([cosine_inv, sine_inv], axis=1)
    lower_block = jnp.concatenate([-sine_inv, cosine_inv], axis=1)
    col_inv = jnp.concatenate([upper_block, lower_block], axis=0).astype(jnp.bfloat16)
    return (col_fwd, row_fwd, row_inv, col_inv)


def kernel_spectra(kernels, kernel_reach, rows_freq, cols_freq):
    tap_count = kernels.shape[-1]
    offsets = jnp.arange(tap_count, dtype=jnp.int32) - kernel_reach
    angle_rows = phase_table(jnp.arange(rows_freq, dtype=jnp.int32), offsets, rows_freq)
    angle_cols = phase_table(jnp.arange(cols_freq, dtype=jnp.int32), offsets, cols_freq)
    cosine_rows = jnp.cos(angle_rows)
    sine_rows = jnp.sin(angle_rows)
    cosine_cols = jnp.cos(angle_cols)
    sine_cols = jnp.sin(angle_cols)
    real_taps = kernels[:, :, 0]
    imag_taps = kernels[:, :, 1]
    highest = lax.Precision.HIGHEST

    def contract(form, first_operand, second_operand):
        return jnp.einsum(form, first_operand, second_operand, precision=highest)

    half_real = contract("ckab,gb->ckag", real_taps, cosine_cols) + contract(
        "ckab,gb->ckag", imag_taps, sine_cols
    )
    half_imag = contract("ckab,gb->ckag", imag_taps, cosine_cols) - contract(
        "ckab,gb->ckag", real_taps, sine_cols
    )
    spec_real = contract("fa,ckag->ckfg", cosine_rows, half_real) + contract(
        "fa,ckag->ckfg", sine_rows, half_imag
    )
    spec_imag = contract("fa,ckag->ckfg", cosine_rows, half_imag) - contract(
        "fa,ckag->ckfg", sine_rows, half_real
    )
    return (spec_real, spec_imag)


def strip_gradient(
    mask_ext, target_strip, col_weight, spec_real, spec_imag, socs_weight, corner_dose, tables
):
    col_fwd, row_fwd, row_inv, col_inv = tables
    ext_rows = mask_ext.shape[0]
    rows_freq = row_fwd.shape[0]
    cols_freq = col_fwd.shape[1] // 2
    strip_rows = row_inv.shape[0]
    width_all = col_fwd.shape[0]
    corner_count, kernel_count = socs_weight.shape
    normalize = 1.0 / (rows_freq * cols_freq)
    along_cols = jnp.dot(mask_ext, col_fwd, preferred_element_type=jnp.float32).astype(jnp.bfloat16)
    swapped = jnp.concatenate([along_cols[:, cols_freq:], -along_cols[:, :cols_freq]], axis=1)
    stacked = jnp.concatenate([along_cols, swapped], axis=0)
    spectrum = jnp.dot(row_fwd, stacked, preferred_element_type=jnp.float32)
    mask_real = spectrum[:, :cols_freq]
    mask_imag = spectrum[:, cols_freq:]
    prod_real = (mask_real * spec_real - mask_imag * spec_imag).astype(jnp.bfloat16)
    prod_imag = (mask_real * spec_imag + mask_imag * spec_real).astype(jnp.bfloat16)
    blocks = jnp.concatenate(
        [
            jnp.concatenate([prod_real, prod_imag], axis=3),
            jnp.concatenate([-prod_imag, prod_real], axis=3),
        ],
        axis=2,
    )
    row_passed = jnp.einsum(
        "jf,ckfg->ckjg", row_inv, blocks, preferred_element_type=jnp.float32
    ).astype(jnp.bfloat16)
    image_field = jnp.dot(
        row_passed.reshape(-1, 2 * cols_freq), col_inv, preferred_element_type=jnp.float32
    )
    image_field = (
        image_field.reshape(corner_count, kernel_count, strip_rows, 2 * width_all) * normalize
    )
    field_real = image_field[..., :width_all]
    field_imag = image_field[..., width_all:]
    weight_wide = socs_weight[:, :, None, None]
    intensity = jnp.sum(weight_wide * (field_real * field_real + field_imag * field_imag), axis=1)
    dose_wide = corner_dose[:, None, None]
    resist = jax.nn.sigmoid(steep * (dose_wide * intensity - thresh))
    missed = resist - target_strip.astype(jnp.float32)[None]
    d_int = (
        2.0
        * loss_scale
        * steep
        * col_weight[None, None, :]
        * missed
        * dose_wide
        * resist
        * (1.0 - resist)
    )
    d_amplitude = 2.0 * weight_wide * d_int[:, None]
    d_field = jnp.concatenate([d_amplitude * field_real, d_amplitude * field_imag], axis=3).astype(
        jnp.bfloat16
    )
    d_inner = (
        jnp.dot(d_field.reshape(-1, 2 * width_all), col_inv.T, preferred_element_type=jnp.float32)
        * normalize
    )
    d_inner = d_inner.astype(jnp.bfloat16).reshape(
        corner_count, kernel_count, strip_rows, 2 * cols_freq
    )
    d_blocks = jnp.einsum("jf,ckjg->ckfg", row_inv, d_inner, preferred_element_type=jnp.float32)
    upper_part = d_blocks[:, :, :rows_freq]
    lower_part = d_blocks[:, :, rows_freq:]
    d_prod_real = upper_part[..., :cols_freq] + lower_part[..., cols_freq:]
    d_prod_imag = upper_part[..., cols_freq:] - lower_part[..., :cols_freq]
    d_mask_real = jnp.sum(d_prod_real * spec_real + d_prod_imag * spec_imag, axis=1)
    d_mask_imag = jnp.sum(d_prod_imag * spec_real - d_prod_real * spec_imag, axis=1)
    d_spec = jnp.concatenate([d_mask_real, d_mask_imag], axis=2).astype(jnp.bfloat16)
    d_stacked = jnp.einsum("fj,cfg->cjg", row_fwd, d_spec, preferred_element_type=jnp.float32)
    top_part = d_stacked[:, :ext_rows]
    bottom_part = d_stacked[:, ext_rows:]
    d_along = jnp.concatenate(
        [
            top_part[..., :cols_freq] - bottom_part[..., cols_freq:],
            top_part[..., cols_freq:] + bottom_part[..., :cols_freq],
        ],
        axis=2,
    ).astype(jnp.bfloat16)
    return jnp.einsum("cjg,hg->jh", d_along, col_fwd, preferred_element_type=jnp.float32)


def per_device(
    mask_logits, target, adam_first, adam_second, tile_counts, kernels, socs_weight, corner_dose
):
    strip_rows = mask_logits.shape[0]
    width_all = target.shape[1]
    kernel_reach = kernels.shape[-1] // 2
    ext_rows = strip_rows + 2 * kernel_reach
    rows_freq = (ext_rows + 7) // 8 * 8
    cols_freq = (width_all + 2 * kernel_reach + 127) // 128 * 128
    tables = dft_tables(strip_rows, kernel_reach, width_all, rows_freq, cols_freq)
    spec_real, spec_imag = kernel_spectra(kernels, kernel_reach, rows_freq, cols_freq)
    counts = tile_counts[0].astype(jnp.float32)
    col_weight = jnp.repeat(counts / (counts + 4.0), width_all // counts.shape[0])
    logits = mask_logits
    first = adam_first
    second = adam_second
    for iteration in range(ITERS):
        opacity = jax.nn.sigmoid(logits)
        mask_bf = opacity.astype(jnp.bfloat16)
        whole_mask = lax.all_gather(mask_bf, "corner", axis=1, tiled=True)
        mask_ext = padded(whole_mask, (("tile", 0),), kernel_reach)
        ext_grad = strip_gradient(
            mask_ext, target, col_weight, spec_real, spec_imag, socs_weight, corner_dose, tables
        )
        summed = lax.psum_scatter(
            ext_grad.astype(jnp.bfloat16), "corner", scatter_dimension=1, tiled=True
        ).astype(jnp.float32)
        from_below = passed_along(summed[:kernel_reach], "tile", -1)
        from_above = passed_along(summed[kernel_reach + strip_rows :], "tile", 1)
        grad_mask = summed[kernel_reach : kernel_reach + strip_rows]
        grad_mask = grad_mask + jnp.pad(from_below, ((strip_rows - kernel_reach, 0), (0, 0)))
        grad_mask = grad_mask + jnp.pad(from_above, ((0, strip_rows - kernel_reach), (0, 0)))
        gradient = grad_mask * opacity * (1.0 - opacity)
        count_now = prior_steps + iteration + 1.0
        first = beta_one * first + (1.0 - beta_one) * gradient
        second = beta_two * second + (1.0 - beta_two) * gradient * gradient
        first_hat = first / (1.0 - beta_one**count_now)
        second_hat = second / (1.0 - beta_two**count_now)
        logits = logits - step_size * first_hat / (jnp.sqrt(second_hat) + adam_eps)
    return (logits, first, second)


def solution(mesh):
    return jax.shard_map(
        per_device,
        mesh=mesh,
        in_specs=(
            P(("grp", "tile"), "corner"),
            P(("grp", "tile"), None),
            P(("grp", "tile"), "corner"),
            P(("grp", "tile"), "corner"),
            P(("grp", "tile"), None),
            P("corner", None, None, None, None),
            P("corner", None),
            P("corner"),
        ),
        out_specs=(
            P(("grp", "tile"), "corner"),
            P(("grp", "tile"), "corner"),
            P(("grp", "tile"), "corner"),
        ),
        check_vma=False,
    )
```

profile of v0, /device:TPU:0, one launch (start us, length us, event | category | flops | bytes accessed | tf_op | source)
XLA Modules:
  0.0 138.1 jit_solution(5183184483789608035)
XLA Ops:
  8.1 2.0 %all_gather.6 = bf16[48,512]{1,0:T(8,128)(2,1)S(1)} all-gather(bf16[48,256]{1,0:T(8,128)(2,1)S(1)} %fusion.186), channel_id=1, replica_groups=mesh['grp'=2,'tile'=8,'corner'=2] {'corner'}, dimensions={1}, use_global_device_ids=true | all-gather | bytes 73728 | tf_op jit(solution)/shard_map/all_gather | solution.py:212
  10.1 4.7 %collective-permute-start = (bf16[17,512]{1,0:T(8,128)(2,1)S(1)}, bf16[17,512]{1,0:T(8,128)(2,1)S(1)}, u32[]{:S(2)}, u32[]{:S(2)}) collective-permute-start(bf16[17,512]{1,0:T(8,128)(2,1)S(1)} %get-tuple-element.37), channel_id=1, source_target_pairs={{0,2},{2,4},{4,6},{6,8},{8,10},{10,12},{12,14},{1,3},{3,5},{5,7},{... | collective-permute-start | bytes 52232 | tf_op jit(solution)/shard_map/ppermute | solution.py:26
  14.8 1.3 collective-permute-start.1
  16.2 5.8 %fusion.51 = bf16[640,512]{1,0:T(8,128)(2,1)} fusion(), kind=kLoop, calls=%fused_computation.88 | loop fusion | flops 3276800 | bytes 655360 | tf_op jit(solution)/shard_map/convert.25
  21.9 5.6 %negate_convert_fusion.1 = (bf16[512,640]{1,0:T(8,128)(2,1)S(1)}, bf16[512,640]{1,0:T(8,128)(2,1)S(1)}) fusion(), kind=kLoop, calls=%fused_computation.89 | loop fusion | flops 3932160 | bytes 1310720 | tf_op jit(solution)/shard_map/convert.29
  27.6 6.7 %negate_convert_fusion = (bf16[640,512]{1,0:T(8,128)(2,1)}, bf16[640,512]{1,0:T(8,128)(2,1)}) fusion(), kind=kLoop, calls=%fused_computation.82 | loop fusion | flops 3932160 | bytes 1310720 | tf_op jit(solution)/shard_map/convert.22
  39.8 1.8 %fusion.175 = f32[8,640,88]{1,2,0:T(8,128)S(1)} fusion(f32[8,35,640]{2,1,0:T(8,128)S(1)} %fusion.57, s32[35]{0:T(128)S(1)} %iota_add_fusion.1), kind=kOutput, calls=%fused_computation.250 | convolution fusion | flops 189262912 | bytes 2519180 | tf_op jit(solution)/shard_map/fa,ckag->ckfg/dot_general | solution.py:92
  41.6 1.8 %fusion.173 = f32[8,640,88]{1,2,0:T(8,128)S(1)} fusion(f32[8,35,640]{2,1,0:T(8,128)S(1)} %fusion.56, s32[35]{0:T(128)S(1)} %iota_add_fusion.1), kind=kOutput, calls=%fused_computation.248 | convolution fusion | flops 189262912 | bytes 2519180 | tf_op jit(solution)/shard_map/fa,ckag->ckfg/dot_general | solution.py:92
  43.4 1.8 %convolution_subtract_fusion = f32[8,640,88]{1,2,0:T(8,128)S(1)} fusion(f32[8,640,88]{1,2,0:T(8,128)S(1)} %fusion.173, f32[8,35,640]{2,1,0:T(8,128)S(1)} %fusion.57, s32[35]{0:T(128)S(1)} %iota_add_fusion.1), kind=kOutput, calls=%fused_computation.75 | convolution fusion | flops 189713472 | bytes 4321420 | tf_op jit(solution)/shard_map/fa,ckag->ckfg/dot_general | solution.py:92
  46.8 3.1 %fusion.25 = (bf16[1,8,88,640]{3,2,1,0:T(8,128)(2,1)}, f32[8,640,88]{1,2,0:T(8,128)S(1)}) fusion(f32[8,640,88]{1,2,0:T(8,128)S(1)} %convolution_subtract_fusion, f32[88,640]{1,0:T(8,128)S(1)} %get-tuple-element.28, f32[88,640]{1,0:T(8,128)S(1)} %get-tuple-element.27, f32[8,640,88]{1,2,0:T(8,128)S(1)} %fusion.175, f32[8,35,640]{2,1,0:T(8,128)S(1)} %fusion.56, ...), kind=kOutput, calls=%fused_computation.50 | convolution fusion | flops 191515712 | bytes 7475340 | tf_op jit(solution)/shard_map/fa,ckag->ckfg/dot_general | solution.py:92
  49.9 1.8 %fusion.247 = (bf16[1,8,88,640]{3,2,1,0:T(8,128)(2,1)}, bf16[1,8,88,640]{3,2,1,0:T(8,128)(2,1)}) fusion(f32[8,640,88]{1,2,0:T(8,128)S(1)} %get-tuple-element.46, f32[88,640]{1,0:T(8,128)S(1)} %get-tuple-element.28, f32[8,640,88]{1,2,0:T(8,128)S(1)} %convolution_subtract_fusion, f32[88,640]{1,0:T(8,128)S(1)} %get-tuple-element.27), kind=kLoop, calls=%fused_computation.315 | loop fusion | flops 2252800 | bytes 5857280 | tf_op jit(solution)/shard_map/neg | solution.py:131
  51.7 4.7 %multiply_bitcast_fusion.1 = f32[1,8,48,1024]{3,2,1,0:T(8,128)S(1)} fusion(bf16[1,8,88,640]{3,2,1,0:T(8,128)(2,1)} %get-tuple-element.45, bf16[1,8,88,640]{3,2,1,0:T(8,128)(2,1)} %get-tuple-element.15, bf16[1,8,88,640]{3,2,1,0:T(8,128)(2,1)} %get-tuple-element.16, bf16[48,88]{1,0:T(8,128)(2,1)S(1)} %get-tuple-element.44, ...), kind=kOutput, calls=%fused_computation.74 | convolution fusion | flops 1205470208 | bytes 6259200 | tf_op jit(solution)/shard_map/dot_general | solution.py:138
  63.8 10.1 %reduce-scatter.3.cloned.1.call-done = bf16[82,256]{1,0:T(8,128)(2,1)} async-done(((bf16[82,512]{1,0:T(8,128)(2,1)}), bf16[82,256]{1,0:T(8,128)(2,1)}) %reduce-scatter.3.cloned.1.call-update) | async-done | bytes 42000 | tf_op jit(solution)/shard_map/reduce_scatter | solution.py:217
  74.6 1.3 collective-permute-start.2
  75.9 4.5 %collective-permute-start.3 = (f32[17,256]{1,0:T(8,128)S(1)}, f32[17,256]{1,0:T(8,128)S(1)}, u32[]{:S(2)}, u32[]{:S(2)}) collective-permute-start(f32[17,256]{1,0:T(8,128)S(1)} %get-tuple-element.42), channel_id=1, source_target_pairs={{0,2},{2,4},{4,6},{6,8},{8,10},{10,12},{12,14},{1,3},{3,5},{5,7},{... | collective-permute-start | bytes 52232 | tf_op jit(solution)/shard_map/ppermute | solution.py:37
  82.7 1.8 %all_gather.7 = bf16[48,512]{1,0:T(8,128)(2,1)S(1)} all-gather(bf16[48,256]{1,0:T(8,128)(2,1)S(1)} %get-tuple-element.12), channel_id=1, replica_groups=mesh['grp'=2,'tile'=8,'corner'=2] {'corner'}, dimensions={1}, use_global_device_ids=true | all-gather | bytes 73728 | tf_op jit(solution)/shard_map/all_gather | solution.py:212
  84.5 4.5 %collective-permute-start.4 = (bf16[17,512]{1,0:T(8,128)(2,1)S(1)}, bf16[17,512]{1,0:T(8,128)(2,1)S(1)}, u32[]{:S(2)}, u32[]{:S(2)}) collective-permute-start(bf16[17,512]{1,0:T(8,128)(2,1)S(1)} %get-tuple-element.35), channel_id=1, source_target_pairs={{0,2},{2,4},{4,6},{6,8},{8,10},{10,12},{12,14},{1,3},{3,5},{5,7},{... | collective-permute-start | bytes 52232 | tf_op jit(solution)/shard_map/ppermute | solution.py:26
  89.0 1.3 collective-permute-start.5
  90.5 5.4 %collective-permute-done.5 = bf16[17,512]{1,0:T(8,128)(2,1)S(1)} collective-permute-done((bf16[17,512]{1,0:T(8,128)(2,1)S(1)}, bf16[17,512]{1,0:T(8,128)(2,1)S(1)}, u32[]{:S(2)}, u32[]{:S(2)}) %collective-permute-start.5) | collective-permute-done | bytes 17440 | tf_op jit(solution)/shard_map/ppermute | solution.py:29
  97.8 1.3 fusion.33
  99.0 1.6 %fusion.244 = (bf16[1,8,88,640]{3,2,1,0:T(8,128)(2,1)}, bf16[1,8,88,640]{3,2,1,0:T(8,128)(2,1)}) fusion(f32[8,640,88]{1,2,0:T(8,128)S(1)} %copy-done.2, f32[88,640]{1,0:T(8,128)S(1)} %get-tuple-element.26, f32[8,640,88]{1,2,0:T(8,128)S(1)} %convolution_subtract_fusion, f32[88,640]{1,0:T(8,128)S(1)} %get-tuple-element.25), kind=kLoop, calls=%fused_computation.314 | loop fusion | flops 2252800 | bytes 5857280 | tf_op jit(solution)/shard_map/neg | solution.py:131
  100.7 4.6 %multiply_bitcast_fusion = f32[1,8,48,1024]{3,2,1,0:T(8,128)S(1)} fusion(bf16[1,8,88,640]{3,2,1,0:T(8,128)(2,1)} %fusion.33, bf16[1,8,88,640]{3,2,1,0:T(8,128)(2,1)} %get-tuple-element.10, bf16[1,8,88,640]{3,2,1,0:T(8,128)(2,1)} %get-tuple-element.11, bf16[48,88]{1,0:T(8,128)(2,1)S(1)} %get-tuple-element.44, bf16[48,88]{1,0:T(8,128)(2,1)S(1)} %get-tuple-element.43, ...), kind=kOutput, calls=%fused_computation.73 | convolution fusion | flops 1205470208 | bytes 6259200 | tf_op jit(solution)/shard_map/dot_general | solution.py:138
  113.3 9.2 %reduce-scatter.5.cloned.1.call-done = bf16[82,256]{1,0:T(8,128)(2,1)} async-done(((bf16[82,512]{1,0:T(8,128)(2,1)}), bf16[82,256]{1,0:T(8,128)(2,1)}) %reduce-scatter.5.cloned.1.call-update) | async-done | bytes 42000 | tf_op jit(solution)/shard_map/reduce_scatter | solution.py:217
  124.5 4.5 %collective-permute-start.7 = (f32[17,256]{1,0:T(8,128)S(1)}, f32[17,256]{1,0:T(8,128)S(1)}, u32[]{:S(2)}, u32[]{:S(2)}) collective-permute-start(f32[17,256]{1,0:T(8,128)S(1)} %get-tuple-element.40), channel_id=1, source_target_pairs={{0,2},{2,4},{4,6},{6,8},{8,10},{10,12},{12,14},{1,3},{3,5},{5,7},{... | collective-permute-start | bytes 52232 | tf_op jit(solution)/shard_map/ppermute | solution.py:37
  (111 shorter events, 31.6 us)
Async XLA Ops:
  7.2 27.1 %copy-start.23 = (f32[1,8]{1,0:T(1,128)S(1)}, f32[1,8]{1,0:T(1,128)}, u32[]{:S(2)}) copy-start(f32[1,8]{1,0:T(1,128)} %param.14) | copy-start | bytes 100
  7.2 27.1 %copy-start.25 = (s32[1,4]{1,0:T(1,128)S(1)}, s32[1,4]{1,0:T(1,128)}, u32[]{:S(2)}) copy-start(s32[1,4]{1,0:T(1,128)} %param.12) | copy-start | bytes 52
  7.2 27.4 %copy-start.16 = (f32[1,8,2,35,35]{4,2,3,1,0:T(2,128)S(1)}, f32[1,8,2,35,35]{4,2,3,1,0:T(2,128)}, u32[]{:S(2)}) copy-start(f32[1,8,2,35,35]{4,2,3,1,0:T(2,128)} %param.13) | copy-start | bytes 235204
  7.2 66.7 %reduce-scatter.3.cloned.1.call-start = ((), (), s32[]{:S(2)}) async-start(), calls=%async_computation.2 | async-start | bytes 135168 | tf_op jit(solution)/shard_map/reduce_scatter | solution.py:217
  10.1 35.9 %collective-permute-start = (bf16[17,512]{1,0:T(8,128)(2,1)S(1)}, bf16[17,512]{1,0:T(8,128)(2,1)S(1)}, u32[]{:S(2)}, u32[]{:S(2)}) collective-permute-start(bf16[17,512]{1,0:T(8,128)(2,1)S(1)} %get-tuple-element.37), channel_id=1, source_target_pairs={{0,2},{2,4},{4,6},{6,8},{8,10},{10,12},{12,14},{1,3},{3,5},{5,7},{... | collective-permute-start | bytes 52232 | tf_op jit(solution)/shard_map/ppermute | solution.py:26
  14.8 31.2 %collective-permute-start.1 = (bf16[17,512]{1,0:T(8,128)(2,1)S(1)}, bf16[17,512]{1,0:T(8,128)(2,1)S(1)}, u32[]{:S(2)}, u32[]{:S(2)}) collective-permute-start(bf16[17,512]{1,0:T(8,128)(2,1)S(1)} %get-tuple-element.38), channel_id=1, source_target_pairs={{2,0},{4,2},{6,4},{8,6},{10,8},{12,10},{14,12},{3,1},{5,3},{7,5},{... | collective-permute-start | bytes 52232 | tf_op jit(solution)/shard_map/ppermute | solution.py:29
  27.5 18.5 %copy-start.4 = (bf16[512,640]{1,0:T(8,128)(2,1)}, bf16[512,640]{1,0:T(8,128)(2,1)S(1)}, u32[]{:S(2)}) copy-start(bf16[512,640]{1,0:T(8,128)(2,1)S(1)} %get-tuple-element.47) | copy-start | bytes 1966084
  27.6 18.5 %copy-start.7 = (bf16[512,640]{1,0:T(8,128)(2,1)}, bf16[512,640]{1,0:T(8,128)(2,1)S(1)}, u32[]{:S(2)}) copy-start(bf16[512,640]{1,0:T(8,128)(2,1)S(1)} %get-tuple-element.48) | copy-start | bytes 1966084
  34.3 22.5 %copy-start.24 = (f32[8]{0:T(128)}, f32[8]{0:T(128)S(1)}, u32[]{:S(2)}) copy-start(f32[8]{0:T(128)S(1)} %broadcast_multiply_fusion) | copy-start | bytes 100
  51.7 5.0 %copy-start.22 = (bf16[48,512]{1,0:T(8,128)(2,1)S(1)}, bf16[48,512]{1,0:T(8,128)(2,1)}, u32[]{:S(2)}) copy-start(bf16[48,512]{1,0:T(8,128)(2,1)} %param.9) | copy-start | bytes 147460
  61.7 20.3 %copy-start.17 = (f32[48,256]{1,0:T(8,128)S(1)}, f32[48,256]{1,0:T(8,128)}, u32[]{:S(2)}) copy-start(f32[48,256]{1,0:T(8,128)} %param.11) | copy-start | bytes 147460
  61.7 20.2 %copy-start.18 = (f32[48,256]{1,0:T(8,128)S(1)}, f32[48,256]{1,0:T(8,128)}, u32[]{:S(2)}) copy-start(f32[48,256]{1,0:T(8,128)} %param.10) | copy-start | bytes 147460
  61.7 20.2 %copy-start.21 = (f32[48,256]{1,0:T(8,128)S(1)}, f32[48,256]{1,0:T(8,128)}, u32[]{:S(2)}) copy-start(f32[48,256]{1,0:T(8,128)} %param.8) | copy-start | bytes 147460
  63.7 58.8 %reduce-scatter.5.cloned.1.call-start = ((), (), s32[]{:S(2)}) async-start(), calls=%async_computation.3 | async-start | bytes 135168 | tf_op jit(solution)/shard_map/reduce_scatter | solution.py:217
  74.6 6.6 %collective-permute-start.2 = (f32[17,256]{1,0:T(8,128)S(1)}, f32[17,256]{1,0:T(8,128)S(1)}, u32[]{:S(2)}, u32[]{:S(2)}) collective-permute-start(f32[17,256]{1,0:T(8,128)S(1)} %get-tuple-element.41), channel_id=1, source_target_pairs={{2,0},{4,2},{6,4},{8,6},{10,8},{12,10},{14,12},{3,1},{5,3},{7,5},{... | collective-permute-start | bytes 52232 | tf_op jit(solution)/shard_map/ppermute | solution.py:37
  75.9 6.1 %collective-permute-start.3 = (f32[17,256]{1,0:T(8,128)S(1)}, f32[17,256]{1,0:T(8,128)S(1)}, u32[]{:S(2)}, u32[]{:S(2)}) collective-permute-start(f32[17,256]{1,0:T(8,128)S(1)} %get-tuple-element.42), channel_id=1, source_target_pairs={{0,2},{2,4},{4,6},{6,8},{8,10},{10,12},{12,14},{1,3},{3,5},{5,7},{... | collective-permute-start | bytes 52232 | tf_op jit(solution)/shard_map/ppermute | solution.py:37
  84.5 6.0 %collective-permute-start.4 = (bf16[17,512]{1,0:T(8,128)(2,1)S(1)}, bf16[17,512]{1,0:T(8,128)(2,1)S(1)}, u32[]{:S(2)}, u32[]{:S(2)}) collective-permute-start(bf16[17,512]{1,0:T(8,128)(2,1)S(1)} %get-tuple-element.35), channel_id=1, source_target_pairs={{0,2},{2,4},{4,6},{6,8},{8,10},{10,12},{12,14},{1,3},{3,5},{5,7},{... | collective-permute-start | bytes 52232 | tf_op jit(solution)/shard_map/ppermute | solution.py:26
  89.0 6.9 %collective-permute-start.5 = (bf16[17,512]{1,0:T(8,128)(2,1)S(1)}, bf16[17,512]{1,0:T(8,128)(2,1)S(1)}, u32[]{:S(2)}, u32[]{:S(2)}) collective-permute-start(bf16[17,512]{1,0:T(8,128)(2,1)S(1)} %get-tuple-element.36), channel_id=1, source_target_pairs={{2,0},{4,2},{6,4},{8,6},{10,8},{12,10},{14,12},{3,1},{5,3},{7,5},{... | collective-permute-start | bytes 52232 | tf_op jit(solution)/shard_map/ppermute | solution.py:29
  105.3 2.1 %copy-start.11 = (bf16[640,512]{1,0:T(8,128)(2,1)S(1)}, bf16[640,512]{1,0:T(8,128)(2,1)}, u32[]{:S(2)}) copy-start(bf16[640,512]{1,0:T(8,128)(2,1)} %fusion.51) | copy-start | bytes 1966084
  105.3 2.1 %copy-start.13 = (bf16[640,512]{1,0:T(8,128)(2,1)S(1)}, bf16[640,512]{1,0:T(8,128)(2,1)}, u32[]{:S(2)}) copy-start(bf16[640,512]{1,0:T(8,128)(2,1)} %get-tuple-element.51) | copy-start | bytes 1966084
  111.3 19.3 %copy-start.19 = (f32[48,256]{1,0:T(8,128)S(1)}, f32[48,256]{1,0:T(8,128)}, u32[]{:S(2)}) copy-start(f32[48,256]{1,0:T(8,128)} %get-tuple-element.13) | copy-start | bytes 147460
  111.3 19.3 %copy-start.20 = (f32[48,256]{1,0:T(8,128)S(1)}, f32[48,256]{1,0:T(8,128)}, u32[]{:S(2)}) copy-start(f32[48,256]{1,0:T(8,128)} %get-tuple-element.14) | copy-start | bytes 147460
  123.2 6.6 %collective-permute-start.6 = (f32[17,256]{1,0:T(8,128)S(1)}, f32[17,256]{1,0:T(8,128)S(1)}, u32[]{:S(2)}, u32[]{:S(2)}) collective-permute-start(f32[17,256]{1,0:T(8,128)S(1)} %get-tuple-element.39), channel_id=1, source_target_pairs={{2,0},{4,2},{6,4},{8,6},{10,8},{12,10},{14,12},{3,1},{5,3},{7,5},{... | collective-permute-start | bytes 52232 | tf_op jit(solution)/shard_map/ppermute | solution.py:37
  124.5 6.1 %collective-permute-start.7 = (f32[17,256]{1,0:T(8,128)S(1)}, f32[17,256]{1,0:T(8,128)S(1)}, u32[]{:S(2)}, u32[]{:S(2)}) collective-permute-start(f32[17,256]{1,0:T(8,128)S(1)} %get-tuple-element.40), channel_id=1, source_target_pairs={{0,2},{2,4},{4,6},{6,8},{8,10},{10,12},{12,14},{1,3},{3,5},{5,7},{... | collective-permute-start | bytes 52232 | tf_op jit(solution)/shard_map/ppermute | solution.py:37
  (12 other events, 17.0 us)
Sparse Core Ops, SparseCore 0:
  63.9 9.9 reduce-scatter.2
  113.5 9.0 reduce-scatter.4
where the time goes:
time: 140 us; the launch traced here: 138 us
  matrix products  31.9 us (23%)
  other arithmetic  31.2 us (22%)
  waiting for transfers between devices  26.3 us (19%)
  starting transfers between devices  23.5 us (17%)
  between operations  15.3 us (11%)
  local copies, waits for them, and re-layouts  6.05 us (4%)
  blocking collectives  3.82 us (3%)
    another operation x7, other arithmetic  19.6 us
    reduce_scatter x2, waiting for transfers between devices, per_device(): lax.psum_scatter(ext_grad.astype(jnp.bfloat16), 'corner', scatter_dimensi...  19.3 us
    dot_general x8, matrix products, contract(): return jnp.einsum(form, first_operand, second_operand, precision=highest)  13.4 us
    ppermute x4, starting transfers between devices, passed_along(): return lax.ppermute(shard, axis, pairs)  11.7 us
    dot_general x2, matrix products, strip_gradient(): jnp.dot(row_passed.reshape(-1, 2 * cols_freq), col_inv, preferred_element...  9.32 us
    ppermute x2, starting transfers between devices, padded(): lax.ppermute(lax.slice_in_dim(block, block.shape[dim] - width, None, axis...  9.21 us
    ppermute x2, waiting for transfers between devices, padded(): lax.ppermute(lax.slice_in_dim(block, 0, width, axis=dim), axis, backward)  5.42 us
    unnamed x52, local copies, waits for them, and re-layouts  4.21 us
  transfers between devices with their start and end apart: 10, of which 6 were waited for; matrix products, arithmetic and copies ran while one was open for 22% of the time, Pallas kernels for 0%

commit v1 on v0

v1 whole, which is shorter than its diff:
```python
import functools
import math

import jax
import jax.numpy as jnp
import numpy as np
from jax import lax
from jax.experimental import pallas as pl
from jax.experimental.pallas import tpu as pltpu
from jax.sharding import PartitionSpec as P

ITERS = 2

steep = 8.0
thresh = 0.5
loss_scale = 20.0
step_size = 0.05
beta_one = 0.9
beta_two = 0.999
adam_eps = 1e-08
prior_steps = 1000.0

LANES = 128
HALF_SPEC = 128
COL_LEN = 2 * HALF_SPEC

BF = jnp.bfloat16
F32 = jnp.float32


def up_to(value, unit):
    return -(-value // unit) * unit


class Plan:
    def __init__(self, strip_rows, width, taps):
        reach = taps // 2
        self.strip_rows, self.width, self.taps, self.reach = strip_rows, width, taps, reach
        self.field_rows = strip_rows + 2 * reach
        self.field_pad = up_to(self.field_rows, 8)
        self.ext_rows = strip_rows + 4 * reach
        self.row_len = up_to(self.ext_rows, 128)
        self.taps_pad = up_to(taps, 8)
        self.col_tiles = width // LANES - 1
        self.starts = [LANES * t for t in range(self.col_tiles)]
        assert width % LANES == 0 and self.col_tiles >= 2
        assert LANES > 4 * reach
        edge = LANES // 2 - 8
        self.bounds = [0] + [s + edge for s in self.starts[1:]] + [width]

        omega = 2.0 * math.pi * (np.arange(HALF_SPEC) + 0.5) / COL_LEN
        phi = 2.0 * math.pi * np.arange(self.row_len) / self.row_len
        rows = np.arange(self.row_len)

        fwd = []
        for t, start in enumerate(self.starts):
            x = start + np.arange(COL_LEN)
            keep = np.ones(COL_LEN)
            if t == 0:
                keep = keep * (x < COL_LEN - reach)
            if t == self.col_tiles - 1:
                keep = keep * (x >= start + reach)
            angle = (x - start)[:, None] * omega[None, :]
            fwd.append(np.concatenate([np.cos(angle), -np.sin(angle)], 1) * keep[:, None])
        self.col_fwd = np.stack(fwd)
        self.col_adj = self.col_fwd.transpose(0, 2, 1)

        scale = 2.0 / (COL_LEN * self.row_len)
        angle = omega[:, None] * np.arange(COL_LEN)[None, :]
        self.col_inv = np.concatenate([np.cos(angle), -np.sin(angle)], 0) * scale
        self.col_inv_adj = self.col_inv.T

        angle = phi[:, None] * rows[None, :]
        live = (rows < self.ext_rows)[None, :]
        c, s = np.cos(angle) * live, np.sin(angle) * live
        self.row_fwd = np.block([[c, s], [-s, c]])
        own = slice(2 * reach, 2 * reach + strip_rows)
        self.row_adj = np.block([[c[:, own].T, -s[:, own].T], [s[:, own].T, c[:, own].T]])

        angle = (np.arange(self.field_pad) + reach)[:, None] * phi[None, :]
        live = (np.arange(self.field_pad) < self.field_rows)[:, None]
        c, s = np.cos(angle) * live, np.sin(angle) * live
        self.row_inv = np.block([[c, -s], [s, c]])
        self.row_inv_adj = self.row_inv.T

        tap = np.arange(taps) - reach
        angle = tap[:, None] * omega[None, :]
        self.tap_cols = np.concatenate([np.cos(angle), -np.sin(angle)], 1)
        angle = phi[:, None] * tap[None, :]
        fill = ((0, 0), (0, self.taps_pad - taps))
        c, s = np.pad(np.cos(angle), fill), np.pad(np.sin(angle), fill)
        self.tap_rows = np.block([[c, s], [-s, c]])


@functools.lru_cache(maxsize=None)
def plan_of(strip_rows, width, taps):
    return Plan(strip_rows, width, taps)


def bf16_table(table):
    return np.asarray(table, np.float32).astype(BF)


def split_table(table):
    high = np.asarray(table, np.float32).astype(BF)
    low = (np.asarray(table, np.float64) - high.astype(np.float64)).astype(np.float32).astype(BF)
    return high, low


def dot(left, right):
    return lax.dot_general(left, right, (((1,), (0,)), ((), ())), preferred_element_type=F32)


def split(value):
    high = value.astype(BF)
    return high, (value - high.astype(F32)).astype(BF)


def spectra_body(plan, weight_ref, kern_ref, cols_hi_ref, cols_lo_ref, rows_ref, out_ref):
    count = kern_ref.shape[0]
    pad = plan.taps_pad - plan.taps
    for k in range(count):
        hi, lo = split(kern_ref[k])
        half = dot(hi, cols_hi_ref[...]) + dot(lo, cols_hi_ref[...]) + dot(hi, cols_lo_ref[...])
        half = jnp.concatenate([half, jnp.zeros((pad, half.shape[1]), F32)], axis=0)
        stacked = jnp.concatenate([half[:, :HALF_SPEC], half[:, HALF_SPEC:]], axis=0)
        hi, lo = split(stacked)
        spec = dot(rows_ref[...], jnp.concatenate([hi, hi, lo], axis=0))
        root = jnp.sqrt(jnp.full((8, LANES), weight_ref[k // 2], F32))[:1]
        out_ref[k] = spec * root


def kernel_spectra(plan, kernels, socs_weight):
    count = kernels.shape[1] * kernels.shape[2]
    taps = kernels.shape[-1]
    cols_hi, cols_lo = split_table(plan.tap_cols)
    rows_hi, rows_lo = split_table(plan.tap_rows)
    rows_all = np.concatenate([rows_hi, rows_lo, rows_hi], axis=1)
    vmem = pl.BlockSpec(memory_space=pltpu.VMEM)
    return pl.pallas_call(
        functools.partial(spectra_body, plan),
        out_shape=jax.ShapeDtypeStruct((count, 2 * plan.row_len, HALF_SPEC), F32),
        in_specs=[pl.BlockSpec(memory_space=pltpu.SMEM)] + [vmem] * 4,
        out_specs=vmem,
        name="spectra",
    )(
        socs_weight[0],
        kernels.reshape(count, taps, taps),
        jnp.asarray(cols_hi),
        jnp.asarray(cols_lo),
        jnp.asarray(rows_all),
    )


def gradient_body(
    plan,
    dose_ref,
    mask_ref,
    target_ref,
    weight_ref,
    spec_ref,
    col_fwd_ref,
    col_adj_ref,
    col_inv_ref,
    col_inv_adj_ref,
    row_fwd_ref,
    row_adj_ref,
    row_inv_ref,
    row_inv_adj_ref,
    out_ref,
    s_ref,
    field_ref,
    light_ref,
    acc_ref,
):
    tiles = plan.col_tiles
    rows = plan.row_len
    fr = plan.field_pad
    g = HALF_SPEC
    count = spec_ref.shape[0]

    along = []
    for t in range(tiles):
        window = mask_ref[:, plan.starts[t] : plan.starts[t] + COL_LEN]
        a = dot(window, col_fwd_ref[t])
        along.append(jnp.concatenate([a[:, :g], a[:, g:]], axis=0).astype(BF))
    s_ref[...] = dot(row_fwd_ref[...], jnp.concatenate(along, axis=1))
    light_ref[...] = jnp.zeros_like(light_ref)
    acc_ref[...] = jnp.zeros_like(acc_ref)

    def forward(pair, carry):
        for part in range(2):
            k = 2 * pair + part
            k_re, k_im = spec_ref[k, :rows], spec_ref[k, rows:]
            prods = []
            for t in range(tiles):
                lane = slice(t * g, t * g + g)
                s_re, s_im = s_ref[:rows, lane], s_ref[rows:, lane]
                p_re = (s_re * k_re - s_im * k_im).astype(BF)
                p_im = (s_re * k_im + s_im * k_re).astype(BF)
                prods.append(jnp.concatenate([p_re, p_im], axis=0))
            passed = dot(row_inv_ref[...], jnp.concatenate(prods, axis=1))
            for t in range(tiles):
                lane = slice(t * g, t * g + g)
                both = jnp.concatenate([passed[:fr, lane], passed[fr:, lane]], axis=1).astype(BF)
                field = dot(both, col_inv_ref[...])
                field_ref[k, t] = field
                light_ref[t] += field * field
        return carry

    lax.fori_loop(0, count // 2, forward, 0)

    dose = dose_ref[0]
    row = lax.broadcasted_iota(jnp.int32, (fr, COL_LEN), 0)
    col = lax.broadcasted_iota(jnp.int32, (fr, COL_LEN), 1)
    reach, strip = plan.reach, plan.strip_rows
    for t in range(tiles):
        lane = slice(plan.starts[t], plan.starts[t] + COL_LEN)
        resist = 1.0 / (1.0 + jnp.exp(-steep * (dose * light_ref[t] - thresh)))
        missed = resist - target_ref[:, lane].astype(F32)
        above, here, below = (weight_ref[i : i + 1, lane] for i in range(3))
        weight = jnp.where(row < reach, above, jnp.where(row < reach + strip, here, below))
        low, high = plan.bounds[t] - plan.starts[t], plan.bounds[t + 1] - plan.starts[t]
        kept = (row < plan.field_rows) & (col >= low) & (col < high)
        weight = jnp.where(kept, weight, 0.0)
        factor = 4.0 * loss_scale * steep * dose
        light_ref[t] = factor * weight * missed * resist * (1.0 - resist)

    def backward(pair, carry):
        for part in range(2):
            k = 2 * pair + part
            inner = []
            for t in range(tiles):
                d_field = (light_ref[t] * field_ref[k, t]).astype(BF)
                d = dot(d_field, col_inv_adj_ref[...])
                inner.append(jnp.concatenate([d[:, :g], d[:, g:]], axis=0).astype(BF))
            d_prod = dot(row_inv_adj_ref[...], jnp.concatenate(inner, axis=1))
            k_re, k_im = spec_ref[k, :rows], spec_ref[k, rows:]
            for t in range(tiles):
                lane = slice(t * g, t * g + g)
                d_re, d_im = d_prod[:rows, lane], d_prod[rows:, lane]
                acc_ref[:rows, lane] += d_re * k_re + d_im * k_im
                acc_ref[rows:, lane] += d_im * k_re - d_re * k_im
        return carry

    lax.fori_loop(0, count // 2, backward, 0)

    d_along = dot(row_adj_ref[...], acc_ref[...].astype(BF))
    parts = []
    for t in range(tiles):
        lane = slice(t * g, t * g + g)
        both = jnp.concatenate([d_along[:strip, lane], d_along[strip:, lane]], axis=1).astype(BF)
        parts.append(dot(both, col_adj_ref[t]))
    blocks = []
    for b in range(plan.width // LANES):
        terms = []
        for t in range(tiles):
            at = b * LANES - plan.starts[t]
            if 0 <= at < COL_LEN:
                terms.append(parts[t][:, at : at + LANES])
        blocks.append(functools.reduce(lambda x, y: x + y, terms))
    out_ref[...] = jnp.concatenate(blocks, axis=1)


def strip_gradient(plan, mask_ext, target_ext, weights, spec, corner_dose):
    tables = [
        jnp.asarray(bf16_table(table))
        for table in (
            plan.col_fwd,
            plan.col_adj,
            plan.col_inv,
            plan.col_inv_adj,
            plan.row_fwd,
            plan.row_adj,
            plan.row_inv,
            plan.row_inv_adj,
        )
    ]
    vmem = pl.BlockSpec(memory_space=pltpu.VMEM)
    count = spec.shape[0]
    spectrum = (2 * plan.row_len, plan.col_tiles * HALF_SPEC)
    image = (plan.col_tiles, plan.field_pad, COL_LEN)
    return pl.pallas_call(
        functools.partial(gradient_body, plan),
        out_shape=jax.ShapeDtypeStruct((plan.strip_rows, plan.width), F32),
        in_specs=[pl.BlockSpec(memory_space=pltpu.SMEM)] + [vmem] * (4 + len(tables)),
        out_specs=vmem,
        scratch_shapes=[
            pltpu.VMEM(spectrum, F32),
            pltpu.VMEM((count,) + image, F32),
            pltpu.VMEM(image, F32),
            pltpu.VMEM(spectrum, F32),
        ],
        name="gradient",
    )(corner_dose, mask_ext, target_ext, weights, spec, *tables)


def ring(value, axis, by):
    length = lax.axis_size(axis)
    return lax.ppermute(value, axis, [(i, (i + by) % length) for i in range(length)])


def other_corner(value):
    return lax.ppermute(value, "corner", [(0, 1), (1, 0)])


def neighbours(top, bottom):
    place = lax.axis_index("tile")
    last = lax.axis_size("tile") - 1
    above = ring(bottom, "tile", 1)
    below = ring(top, "tile", -1)
    zero = jnp.zeros((), top.dtype)
    return jnp.where(place == 0, zero, above), jnp.where(place == last, zero, below)


def per_device(
    mask_logits, target, adam_first, adam_second, tile_counts, kernels, socs_weight, corner_dose
):
    strip_rows, half_width = mask_logits.shape
    width = target.shape[1]
    plan = plan_of(strip_rows, width, kernels.shape[-1])
    reach = plan.reach
    halo = 2 * reach
    corner = lax.axis_index("corner")

    def whole(own, other):
        left = jnp.where(corner == 0, own, other)
        right = jnp.where(corner == 0, other, own)
        return jnp.concatenate([left, right], axis=-1)

    def own_half(value):
        return jnp.where(corner == 0, value[..., :half_width], value[..., half_width:])

    state = jnp.stack([mask_logits, adam_first, adam_second])
    state = whole(state, other_corner(state))
    logits, first, second = state[0], state[1], state[2]
    opacity = jax.nn.sigmoid(logits)
    mask_bf = opacity.astype(BF)
    counts = jnp.repeat(tile_counts.astype(F32), width // tile_counts.shape[1], axis=1)

    counts_bf = counts.astype(BF)
    above, below = neighbours(
        jnp.concatenate([mask_bf[:halo], target[:reach], counts_bf], axis=0),
        jnp.concatenate([mask_bf[-halo:], target[-reach:], counts_bf], axis=0),
    )
    spec = kernel_spectra(plan, kernels, socs_weight)

    def extended(above_rows, own, below_rows, total):
        have = above_rows.shape[0] + own.shape[0] + below_rows.shape[0]
        blank = jnp.zeros((total - have, own.shape[1]), own.dtype)
        return jnp.concatenate([above_rows, own, below_rows, blank], axis=0)

    target_ext = extended(
        above[halo : halo + reach], target, below[halo : halo + reach], plan.field_pad
    )
    near = jnp.concatenate([above[halo + reach :].astype(F32), counts, below[halo + reach :].astype(F32)])
    near = jnp.pad(near, ((0, 5), (0, 0)))
    weights = near / (near + 4.0)
    above, below = above[:halo], below[:halo]

    for iteration in range(ITERS):
        if iteration:
            opacity = jax.nn.sigmoid(logits)
            mask_bf = opacity.astype(BF)
            above, below = neighbours(mask_bf[:halo], mask_bf[-halo:])
        mask_ext = extended(above, mask_bf, below, plan.row_len)
        partial = strip_gradient(plan, mask_ext, target_ext, weights, spec, corner_dose)
        if iteration < ITERS - 1:
            summed = partial + other_corner(partial.astype(BF)).astype(F32)
        else:
            mine = own_half(partial)
            theirs = jnp.where(corner == 0, partial[:, half_width:], partial[:, :half_width])
            summed = mine + other_corner(theirs.astype(BF)).astype(F32)
            opacity, logits = own_half(opacity), own_half(logits)
            first, second = own_half(first), own_half(second)
        gradient = summed * opacity * (1.0 - opacity)
        count_now = prior_steps + iteration + 1.0
        first = beta_one * first + (1.0 - beta_one) * gradient
        second = beta_two * second + (1.0 - beta_two) * gradient * gradient
        first_hat = first / (1.0 - beta_one**count_now)
        second_hat = second / (1.0 - beta_two**count_now)
        logits = logits - step_size * first_hat / (jnp.sqrt(second_hat) + adam_eps)
    return (logits, first, second)


def solution(mesh):
    return jax.shard_map(
        per_device,
        mesh=mesh,
        in_specs=(
            P(("grp", "tile"), "corner"),
            P(("grp", "tile"), None),
            P(("grp", "tile"), "corner"),
            P(("grp", "tile"), "corner"),
            P(("grp", "tile"), None),
            P("corner", None, None, None, None),
            P("corner", None),
            P("corner"),
        ),
        out_specs=(
            P(("grp", "tile"), "corner"),
            P(("grp", "tile"), "corner"),
            P(("grp", "tile"), "corner"),
        ),
        check_vma=False,
    )
```

time: 140 us -> 63.4 us (0.45)
  matrix products: 31.9 us -> 0 us
  Pallas kernels: 0 us -> 31.4 us
  other arithmetic: 31.2 us -> 9.59 us
  waiting for transfers between devices: 26.3 us -> 6.1 us
  between operations: 15.3 us -> 1.43 us
  starting transfers between devices: 23.5 us -> 11.5 us
  blocking collectives: 3.82 us -> 0 us
  local copies, waits for them, and re-layouts: 6.05 us -> 2.77 us
    dot_general x22 -> x0, matrix products: 31.9 us -> none  [the longest x8 13.4 us: contract(): return jnp.einsum(form, first_operand, second_operand, precision=highest)]
    pallas_call x0 -> x3, Pallas kernels: none -> 31.4 us  [the longest x2 26.9 us: strip_gradient(): pl.pallas_call(functools.partial(gradient_body, plan), out_shape=jax.Shap...]
    reduce_scatter x2 -> x0, waiting for transfers between devices: 19.3 us -> none  [per_device(): lax.psum_scatter(ext_grad.astype(jnp.bfloat16), 'corner', scatter_dimensi...]
    another operation x7 -> x1, other arithmetic: 19.6 us -> 0.86 us  [per_device(): state = jnp.stack([mask_logits, adam_first, adam_second])]
    ppermute x8 -> x7, starting transfers between devices: 23.5 us -> 11.5 us  [the longest x4 10.9 us: ring(): lax.ppermute(value, axis, [(i, (i + by) % length) for i in range(length)])]
    all_gather x2 -> x0, blocking collectives: 3.82 us -> none  [per_device(): whole_mask = lax.all_gather(mask_bf, 'corner', axis=1, tiled=True)]
    neg x2 -> x0, other arithmetic: 3.45 us -> none  [strip_gradient(): -prod_imag]
    unnamed x52 -> x3, local copies, waits for them, and re-layouts: 4.21 us -> 1.72 us
  transfers between devices with their start and end apart: 10 -> 7, of which waited for: 6 -> 4; matrix products, arithmetic and copies ran while one was open for 22% -> 5% of each run, Pallas kernels for 0% -> 7%
where the time goes in v1:
time: 63.4 us; the launch traced here: 62.8 us
  Pallas kernels  31.4 us (50%)
  starting transfers between devices  11.5 us (18%)
  other arithmetic  9.59 us (15%)
  waiting for transfers between devices  6.1 us (10%)
  local copies, waits for them, and re-layouts  2.77 us (4%)
  between operations  1.43 us (2%)
    pallas_call x2, Pallas kernels, strip_gradient(): pl.pallas_call(functools.partial(gradient_body, plan), out_shape=jax.Shap...  26.9 us
    ppermute x4, starting transfers between devices, ring(): lax.ppermute(value, axis, [(i, (i + by) % length) for i in range(length)])  10.9 us
    pallas_call x1, Pallas kernels, kernel_spectra(): pl.pallas_call(functools.partial(spectra_body, plan), out_shape=jax.Shape...  4.58 us
    ppermute x4, waiting for transfers between devices, ring(): lax.ppermute(value, axis, [(i, (i + by) % length) for i in range(length)])  3.69 us
    ppermute x3, waiting for transfers between devices, other_corner(): return lax.ppermute(value, 'corner', [(0, 1), (1, 0)])  2.41 us
    concatenate x3, other arithmetic, extended(): return jnp.concatenate([above_rows, own, below_rows, blank], axis=0)  2.18 us
    unnamed x3, local copies, waits for them, and re-layouts  1.72 us
    sub x1, other arithmetic, per_device(): logits = logits - step_size * first_hat / (jnp.sqrt(second_hat) + adam_eps)  1.5 us
  transfers between devices with their start and end apart: 7, of which 4 were waited for; matrix products, arithmetic and copies ran while one was open for 5% of the time, Pallas kernels for 7%

profile of v1, /device:TPU:0, one launch (start us, length us, event | category | flops | bytes accessed | tf_op | source)
XLA Modules:
  0.0 62.8 jit_solution(13161999666596202089)
XLA Ops:
  0.6 0.9 %pad_maximum_fusion = f32[3,48,256]{2,1,0:T(8,128)S(1)} fusion(f32[1,48,256]{2,1,0:T(8,128)} %bitcast.22, f32[1,48,256]{2,1,0:T(8,128)} %bitcast.24, f32[1,48,256]{2,1,0:T(8,128)} %bitcast.26), kind=kLoop, calls=%fused_computation.5 | loop fusion | flops 73728 | bytes 294912 | tf_op jit(solution)/shard_map/stack | solution.py:334
  2.0 0.7 %convert_bitcast_fusion = f32[4]{0:T(128)S(1)} fusion(s32[1,4]{1,0:T(1,128)} %param.31), kind=kLoop, calls=%fused_computation.50 | loop fusion | flops 4 | bytes 32 | tf_op jit(solution)/shard_map/convert_element_type | solution.py:339
  2.8 0.8 %fusion.23 = (bf16[17,512]{1,0:T(8,128)(2,1)S(1)}, bf16[17,512]{1,0:T(8,128)(2,1)S(1)}) fusion(bf16[48,512]{1,0:T(8,128)(2,1)} %param.28), kind=kLoop, calls=%fused_computation.54 | loop fusion | bytes 69632 | tf_op jit(solution)/shard_map/slice | solution.py:344
  3.6 0.9 %broadcast_select_fusion.1 = (f32[3,48,256]{2,1,0:T(8,128)S(1)}, f32[3,48,256]{2,1,0:T(8,128)S(1)}) fusion(f32[3,48,256]{2,1,0:T(8,128)S(1)} %collective-permute-done, pred[]{:T(512)S(6)} %eq.6, f32[1,48,256]{2,1,0:T(8,128)} %bitcast.23, f32[1,48,256]{2,1,0:T(8,128)} %bitcast.25, f32[1,48,256]{2,1,0:T(8,128)} %bitcast.27), kind=kLoop, calls=%fused_computation.27 | loop fusion | flops 147456 | bytes 589825 | tf_op jit(solution)/shard_map/jit(_where)/select_n | solution.py:327
  4.5 2.5 %collective-permute-start.1 = (bf16[52,512]{1,0:T(8,128)(2,1)S(1)}, bf16[52,512]{1,0:T(8,128)(2,1)S(1)}, u32[]{:S(2)}, u32[]{:S(2)}) collective-permute-start(bf16[52,512]{1,0:T(8,128)(2,1)S(1)} %get-tuple-element.21), channel_id=1, source_target_pairs={{0,2},{2,4},{4,6},{6,8},{8,10},{10,12},{12,14},{14,0},{1,3},{3,5},... | collective-permute-start | bytes 159752 | tf_op jit(solution)/shard_map/ppermute | solution.py:300
  7.9 1.7 %copy.30 = f32[1,8,2,35,35]{4,3,2,1,0:T(8,128)} copy(f32[1,8,2,35,35]{4,2,3,1,0:T(2,128)} %param.32) | data formatting | bytes 156800 | tf_op args[5]
  9.6 4.6 %spectra.1.spec_ref = f32[16,256,128]{2,1,0:T(8,128)} custom-call(f32[8]{0:T(128)} %bitcast.30, f32[16,35,35]{2,1,0:T(8,128)} %bitcast.21, bf16[35,256]{1,0:T(8,128)(2,1)} %constant.24.clone.cols_hi_ref, bf16[35,256]{1,0:T(8,128)(2,1)} %constant.25.clone.cols_lo_ref, bf16[256,240]{1,0:T(8,128)(2,1)} %constant.26.clone.rows_ref), custom_call_target="tpu_custom_call" | custom-call | tf_op jit(solution)/shard_map/spectra/pallas_call | solution.py:140
  14.2 3.1 %collective-permute-start.2 = (bf16[52,512]{1,0:T(8,128)(2,1)S(1)}, bf16[52,512]{1,0:T(8,128)(2,1)S(1)}, u32[]{:S(2)}, u32[]{:S(2)}) collective-permute-start(bf16[52,512]{1,0:T(8,128)(2,1)S(1)} %get-tuple-element.22), channel_id=1, source_target_pairs={{0,14},{2,0},{4,2},{6,4},{8,6},{10,8},{12,10},{14,12},{1,15},{3,1}... | collective-permute-start | bytes 159752 | tf_op jit(solution)/shard_map/ppermute | solution.py:300
  17.3 1.8 %collective-permute-done.2 = bf16[52,512]{1,0:T(8,128)(2,1)S(1)} collective-permute-done((bf16[52,512]{1,0:T(8,128)(2,1)S(1)}, bf16[52,512]{1,0:T(8,128)(2,1)S(1)}, u32[]{:S(2)}, u32[]{:S(2)}) %collective-permute-start.2) | collective-permute-done | bytes 53280 | tf_op jit(solution)/shard_map/ppermute | solution.py:300
  19.1 0.6 add_divide_fusion.2.weight_ref
  19.8 0.7 %maximum_maximum_fusion.mask_ref = bf16[128,512]{1,0:T(8,128)(2,1)} fusion(bf16[34,512]{1,0:T(8,128)(2,1)S(1)} %slice.109, bf16[48,512]{1,0:T(8,128)(2,1)S(1)} %get-tuple-element.11, bf16[34,512]{1,0:T(8,128)(2,1)S(1)} %slice.107, bf16[128]{0:T(256)(128)(2,1)S(1)} %pad.19.clone), kind=kLoop, calls=%fused_computation.6 | loop fusion | flops 524288 | bytes 250112 | tf_op jit(solution)/shard_map/concatenate | solution.py:351
  20.5 0.7 %maximum_maximum_fusion.2.target_ref = bf16[88,512]{1,0:T(8,128)(2,1)} fusion(bf16[17,512]{1,0:T(8,128)(2,1)S(1)} %slice.111, bf16[48,512]{1,0:T(8,128)(2,1)S(1)} %copy-done, bf16[17,512]{1,0:T(8,128)(2,1)S(1)} %slice.110, bf16[88]{0:T(256)(128)(2,1)S(1)} %pad.15.clone), kind=kLoop, calls=%fused_computation.22 | loop fusion | flops 360448 | bytes 174256 | tf_op jit(solution)/shard_map/concatenate | solution.py:351
  21.2 13.4 %gradient.2 = f32[48,512]{1,0:T(8,128)} custom-call(f32[1]{0:T(128)S(6)} %copy.31.dose_ref, bf16[128,512]{1,0:T(8,128)(2,1)} %maximum_maximum_fusion.mask_ref, bf16[88,512]{1,0:T(8,128)(2,1)} %maximum_maximum_fusion.2.target_ref, f32[8,512]{1,0:T(8,128)} %add_divide_fusion.2.weight_ref, f32[16,256,128]{2,1,0:T(8,128)} %spectra.1.spec_ref, ...), custom_call_target="tpu_custom_call" | custom-call | tf_op jit(solution)/shard_map/gradient/pallas_call | solution.py:283
  34.7 0.9 %convert_element_type.48 = bf16[48,512]{1,0:T(8,128)(2,1)S(1)} convert(f32[48,512]{1,0:T(8,128)} %gradient.2) | non-fusion elementwise | flops 24576 | bytes 147456 | tf_op jit(solution)/shard_map/convert_element_type | solution.py:369
  35.6 1.2 %collective-permute-done.3 = bf16[48,512]{1,0:T(8,128)(2,1)S(1)} collective-permute-done((bf16[48,512]{1,0:T(8,128)(2,1)S(1)}, bf16[48,512]{1,0:T(8,128)(2,1)S(1)}, u32[]{:S(2)}, u32[]{:S(2)}) %collective-permute-start.3) | collective-permute-done | bytes 49184 | tf_op jit(solution)/shard_map/ppermute | solution.py:304
  36.8 1.0 %fusion.17 = (bf16[48,512]{1,0:T(8,128)(2,1)S(1)}, f32[48,512]{1,0:T(8,128)S(1)}, f32[48,512]{1,0:T(8,128)S(1)}, f32[48,512]{1,0:T(8,128)S(1)}, f32[48,512]{1,0:T(8,128)S(1)}) fusion(f32[48,512]{1,0:T(8,128)S(1)} %get-tuple-element.12, f32[48,512]{1,0:T(8,128)} %gradient.2, bf16[48,512]{1,0:T(8,128)(2,1)S(1)} %collective-permute-done.3, ...), kind=kLoop, calls=%fused_computation.51 | loop fusion | flops 638976 | bytes 983040 | tf_op jit(solution)/shard_map/convert_element_type | solution.py:364
  37.8 1.8 %collective-permute-start.4 = (bf16[34,512]{1,0:T(8,128)(2,1)S(1)}, bf16[34,512]{1,0:T(8,128)(2,1)S(1)}, u32[]{:S(2)}, u32[]{:S(2)}) collective-permute-start(bf16[34,512]{1,0:T(8,128)(2,1)S(1)} %get-tuple-element.15), channel_id=1, source_target_pairs={{0,2},{2,4},{4,6},{6,8},{8,10},{10,12},{12,14},{14,0},{1,3},{3,5},... | collective-permute-start | bytes 104456 | tf_op jit(solution)/shard_map/ppermute | solution.py:300
  39.6 3.5 %collective-permute-start.5 = (bf16[34,512]{1,0:T(8,128)(2,1)S(1)}, bf16[34,512]{1,0:T(8,128)(2,1)S(1)}, u32[]{:S(2)}, u32[]{:S(2)}) collective-permute-start(bf16[34,512]{1,0:T(8,128)(2,1)S(1)} %get-tuple-element.16), channel_id=1, source_target_pairs={{0,14},{2,0},{4,2},{6,4},{8,6},{10,8},{12,10},{14,12},{1,15},{3,1}... | collective-permute-start | bytes 104456 | tf_op jit(solution)/shard_map/ppermute | solution.py:300
  43.1 1.9 %collective-permute-done.4 = bf16[34,512]{1,0:T(8,128)(2,1)S(1)} collective-permute-done((bf16[34,512]{1,0:T(8,128)(2,1)S(1)}, bf16[34,512]{1,0:T(8,128)(2,1)S(1)}, u32[]{:S(2)}, u32[]{:S(2)}) %collective-permute-start.4) | collective-permute-done | bytes 34848 | tf_op jit(solution)/shard_map/ppermute | solution.py:300
  45.1 0.7 %maximum_maximum_fusion.1.mask_ref = bf16[128,512]{1,0:T(8,128)(2,1)} fusion(bf16[34,512]{1,0:T(8,128)(2,1)S(1)} %broadcast_select_fusion.4, bf16[48,512]{1,0:T(8,128)(2,1)S(1)} %get-tuple-element.6, bf16[34,512]{1,0:T(8,128)(2,1)S(1)} %broadcast_select_fusion.5, bf16[128]{0:T(256)(128)(2,1)S(1)} %pad.19.clone), kind=kLoop, calls=%fused_computation.7 | loop fusion | flops 524288 | bytes 250112 | tf_op jit(solution)/shard_map/concatenate | solution.py:351
  45.8 13.4 %gradient.3 = f32[48,512]{1,0:T(8,128)} custom-call(f32[1]{0:T(128)S(6)} %copy.31.dose_ref, bf16[128,512]{1,0:T(8,128)(2,1)} %maximum_maximum_fusion.1.mask_ref, bf16[88,512]{1,0:T(8,128)(2,1)} %maximum_maximum_fusion.2.target_ref, f32[8,512]{1,0:T(8,128)} %add_divide_fusion.2.weight_ref, f32[16,256,128]{2,1,0:T(8,128)} %spectra.1.spec_ref, ...), custom_call_target="tpu_custom_call" | custom-call | tf_op jit(solution)/shard_map/gradient/pallas_call | solution.py:283
  59.3 0.8 %select_convert_fusion = bf16[48,256]{1,0:T(8,128)(2,1)S(1)} fusion(f32[48,512]{1,0:T(8,128)} %gradient.3, pred[]{:T(512)S(6)} %eq.6), kind=kLoop, calls=%fused_computation.40 | loop fusion | flops 12288 | bytes 73729 | tf_op jit(solution)/shard_map/convert_element_type | solution.py:373
  60.1 1.2 %collective-permute-done.6 = bf16[48,256]{1,0:T(8,128)(2,1)S(1)} collective-permute-done((bf16[48,256]{1,0:T(8,128)(2,1)S(1)}, bf16[48,256]{1,0:T(8,128)(2,1)S(1)}, u32[]{:S(2)}, u32[]{:S(2)}) %collective-permute-start.6) | collective-permute-done | bytes 24608 | tf_op jit(solution)/shard_map/ppermute | solution.py:304
  61.3 1.5 %fusion.13 = (f32[48,256]{1,0:T(8,128)}, f32[48,256]{1,0:T(8,128)}, f32[48,256]{1,0:T(8,128)}) fusion(f32[48,512]{1,0:T(8,128)S(1)} %get-tuple-element.8, pred[]{:T(512)S(6)} %eq.6, f32[48,512]{1,0:T(8,128)S(1)} %get-tuple-element.9, f32[48,512]{1,0:T(8,128)S(1)} %get-tuple-element.10, f32[48,512]{1,0:T(8,128)S(1)} %get-tuple-element.7, ...), kind=kLoop, calls=%fused_computation.38 | loop fusion | flops 270336 | bytes 663553 | tf_op jit(solution)/shard_map/sub | solution.py:382
  (28 shorter events, 1.0 us)
Async XLA Ops:
  1.5 2.1 %collective-permute-start = (f32[3,48,256]{2,1,0:T(8,128)S(1)}, f32[3,48,256]{2,1,0:T(8,128)S(1)}, u32[]{:S(2)}, u32[]{:S(2)}) collective-permute-start(f32[3,48,256]{2,1,0:T(8,128)S(1)} %pad_maximum_fusion), channel_id=1, source_target_pairs={{0,1},{1,0},{2,3},{3,2},{4,5},{5,4},{6,7},{7,6},{8,9},{9,8},{10,11... | collective-permute-start | bytes 442376 | tf_op jit(solution)/shard_map/ppermute | solution.py:304
  4.5 16.0 %copy-start = (bf16[48,512]{1,0:T(8,128)(2,1)S(1)}, bf16[48,512]{1,0:T(8,128)(2,1)}, u32[]{:S(2)}) copy-start(bf16[48,512]{1,0:T(8,128)(2,1)} %param.28) | copy-start | bytes 147460
  4.5 12.7 %collective-permute-start.1 = (bf16[52,512]{1,0:T(8,128)(2,1)S(1)}, bf16[52,512]{1,0:T(8,128)(2,1)S(1)}, u32[]{:S(2)}, u32[]{:S(2)}) collective-permute-start(bf16[52,512]{1,0:T(8,128)(2,1)S(1)} %get-tuple-element.21), channel_id=1, source_target_pairs={{0,2},{2,4},{4,6},{6,8},{8,10},{10,12},{12,14},{14,0},{1,3},{3,5},... | collective-permute-start | bytes 159752 | tf_op jit(solution)/shard_map/ppermute | solution.py:300
  14.2 4.9 %collective-permute-start.2 = (bf16[52,512]{1,0:T(8,128)(2,1)S(1)}, bf16[52,512]{1,0:T(8,128)(2,1)S(1)}, u32[]{:S(2)}, u32[]{:S(2)}) collective-permute-start(bf16[52,512]{1,0:T(8,128)(2,1)S(1)} %get-tuple-element.22), channel_id=1, source_target_pairs={{0,14},{2,0},{4,2},{6,4},{8,6},{10,8},{12,10},{14,12},{1,15},{3,1}... | collective-permute-start | bytes 159752 | tf_op jit(solution)/shard_map/ppermute | solution.py:300
  35.6 1.2 %collective-permute-start.3 = (bf16[48,512]{1,0:T(8,128)(2,1)S(1)}, bf16[48,512]{1,0:T(8,128)(2,1)S(1)}, u32[]{:S(2)}, u32[]{:S(2)}) collective-permute-start(bf16[48,512]{1,0:T(8,128)(2,1)S(1)} %convert_element_type.48), channel_id=1, source_target_pairs={{0,1},{1,0},{2,3},{3,2},{4,5},{5,4},{6,7},{7,6},{8,9},{9,8},{10,11... | collective-permute-start | bytes 147464 | tf_op jit(solution)/shard_map/ppermute | solution.py:304
  37.8 7.2 %collective-permute-start.4 = (bf16[34,512]{1,0:T(8,128)(2,1)S(1)}, bf16[34,512]{1,0:T(8,128)(2,1)S(1)}, u32[]{:S(2)}, u32[]{:S(2)}) collective-permute-start(bf16[34,512]{1,0:T(8,128)(2,1)S(1)} %get-tuple-element.15), channel_id=1, source_target_pairs={{0,2},{2,4},{4,6},{6,8},{8,10},{10,12},{12,14},{14,0},{1,3},{3,5},... | collective-permute-start | bytes 104456 | tf_op jit(solution)/shard_map/ppermute | solution.py:300
  39.6 5.4 %collective-permute-start.5 = (bf16[34,512]{1,0:T(8,128)(2,1)S(1)}, bf16[34,512]{1,0:T(8,128)(2,1)S(1)}, u32[]{:S(2)}, u32[]{:S(2)}) collective-permute-start(bf16[34,512]{1,0:T(8,128)(2,1)S(1)} %get-tuple-element.16), channel_id=1, source_target_pairs={{0,14},{2,0},{4,2},{6,4},{8,6},{10,8},{12,10},{14,12},{1,15},{3,1}... | collective-permute-start | bytes 104456 | tf_op jit(solution)/shard_map/ppermute | solution.py:300
  60.1 1.2 %collective-permute-start.6 = (bf16[48,256]{1,0:T(8,128)(2,1)S(1)}, bf16[48,256]{1,0:T(8,128)(2,1)S(1)}, u32[]{:S(2)}, u32[]{:S(2)}) collective-permute-start(bf16[48,256]{1,0:T(8,128)(2,1)S(1)} %select_convert_fusion), channel_id=1, source_target_pairs={{0,1},{1,0},{2,3},{3,2},{4,5},{5,4},{6,7},{7,6},{8,9},{9,8},{10,11... | collective-permute-start | bytes 73736 | tf_op jit(solution)/shard_map/ppermute | solution.py:304
